TPU v7x, 32 devices: a whole 2x2x4 slice. The times are simulated.
32 devices in a mesh: grp: 4 (over z), ori: 8 (over y, x, core).
Axes of the slice: x: 2, y: 2, z: 4, core: 2. Of those that a mesh axis runs over, the one named last changes fastest.
Arguments:
- particles: bfloat16 [1024, 16640], P(('grp', 'ori')), may hold values from -8 to 8
- priors: int32 [1024, 2], P(('grp', 'ori')), may hold values from 0 to 7, all different within a row; in each aligned block of 32 rows (0 to 31, 32 to 63, ...) at most 16 rows name the same one
- offsets: int32 [2, 1024], P(None, ('grp', 'ori')), may hold values from -2 to 2
- classes: int32 [1024], P(('grp', 'ori')), may hold values from 0 to 15
- ctf_table: float32 [16, 8320], replicated, may hold values from 0.2 to 1
- references: bfloat16 [128, 16640], P('ori'), may hold values from -5 to 5
Outputs:
- back_sum: float32 [128, 16640], P('ori', 'grp')
- ctf_weight: float32 [128, 8320], P('ori', 'grp')
- log_evidence: float32 [1024], P(('grp', 'ori'))
Inputs may be any that keep to these rules, and one draw needn't show every extreme that they name: `priors`: each particle names 2 different orientation blocks. The 32 rows of one device name any one block at most 16 times, and some block is named exactly 16 times by the rows of some devices.
All inputs are finite; a program needn't handle non-finite values.
Results may differ from a plain program's by a relative error of at most 0.0052.
Values may be sent and summed in bfloat16 or wider, within the bound.
A program may use at most 64 MiB of HBM per device.

v0:
```python
import math

import jax
import jax.numpy as jnp
from jax import lax
from jax.sharding import PartitionSpec as P

PX = 128
PY = 65
BOX = 320
SIDE = 8
NSHIFT = 64


two_pi = 2.0 * math.pi
shift_block = 4


def frequencies():
    row_ids = jnp.arange(PX)
    freq_x = jnp.where(row_ids < PX // 2, row_ids, row_ids - PX).astype(jnp.float32)
    freq_y = jnp.arange(PY).astype(jnp.float32)
    return (jnp.repeat(freq_x, PY), jnp.tile(freq_y, PX))


def phases(shift_x, shift_y):
    freq_x, freq_y = frequencies()
    angle_grid = (
        two_pi * (shift_x[:, None] * freq_x[None, :] + shift_y[:, None] * freq_y[None, :]) / BOX
    )
    return (jnp.cos(angle_grid), jnp.sin(angle_grid))


def grid_shifts(first_shift, shift_count):
    shift_ids = first_shift + jnp.arange(shift_count)
    return (
        (shift_ids // SIDE - SIDE // 2).astype(jnp.float32),
        (shift_ids % SIDE - SIDE // 2).astype(jnp.float32),
    )


def kernels(references, first_shift):
    pixel_count = PX * PY
    cosine, sine_table = phases(*grid_shifts(first_shift, shift_block))
    real_part = references[:, :pixel_count].astype(jnp.float32)
    imag_part = references[:, pixel_count:].astype(jnp.float32)
    left_half = cosine[:, None, :] * real_part[None] - sine_table[:, None, :] * imag_part[None]
    right_half = sine_table[:, None, :] * real_part[None] + cosine[:, None, :] * imag_part[None]
    joined = jnp.concatenate([left_half, right_half], axis=-1)
    return joined.reshape(shift_block * references.shape[0], 2 * pixel_count).astype(jnp.bfloat16)


def score_rows(slot_rows, references):
    n_blocks = NSHIFT // shift_block
    score_scale = 2.0 / math.sqrt(PX * PY)

    def one_block(block_id):
        kernel_rows = kernels(references, block_id * shift_block)
        return jnp.dot(slot_rows, kernel_rows.T, preferred_element_type=jnp.float32)

    stacked = lax.map(one_block, jnp.arange(n_blocks))
    return jnp.transpose(stacked, (1, 0, 2)).reshape(slot_rows.shape[0], -1) * score_scale


def slot_positions(prior_rows, n_dest, capacity):
    dest_ids = prior_rows.reshape(-1)
    dest_hits = (dest_ids[:, None] == jnp.arange(n_dest)[None, :]).astype(jnp.int32)
    earlier = jnp.cumsum(dest_hits, axis=0) - dest_hits
    slot_ids = jnp.sum(earlier * dest_hits, axis=1)
    return dest_ids * capacity + slot_ids


def combine_stats(peaks, totals):
    top_peak = jnp.max(peaks, axis=-1)
    return top_peak + jnp.log(jnp.sum(totals * jnp.exp(peaks - top_peak[..., None]), axis=-1))


def centered(particles, offsets, classes, ctf_table):
    pixel_count = PX * PY
    class_picks = (classes[:, None] == jnp.arange(ctf_table.shape[0])[None, :]).astype(jnp.float32)
    ctf_rows = jnp.dot(class_picks, ctf_table, precision=lax.Precision.HIGHEST)
    cosine, sine_table = phases(offsets[0].astype(jnp.float32), offsets[1].astype(jnp.float32))
    real_part = particles[:, :pixel_count].astype(jnp.float32)
    imag_part = particles[:, pixel_count:].astype(jnp.float32)
    return jnp.concatenate(
        [
            ctf_rows * (real_part * cosine + imag_part * sine_table),
            ctf_rows * (imag_part * cosine - real_part * sine_table),
        ],
        axis=-1,
    ).astype(jnp.bfloat16)


def per_device(particles, priors, offsets, classes, ctf_table, references):
    n_ori = lax.axis_size("ori")
    part_count, top_count = priors.shape
    capacity = 2 * part_count * top_count // n_ori
    n_slots = n_ori * capacity
    pixel_count = PX * PY
    refs_dev = references.shape[0]
    n_blocks = NSHIFT // shift_block
    shifted = centered(particles, offsets, classes, ctf_table)
    position = slot_positions(priors, n_ori, capacity)
    routing = (position[None, :] == jnp.arange(n_slots)[:, None]).astype(jnp.int32)
    routing = jnp.sum(routing.reshape(n_slots, part_count, top_count), axis=2)
    send_rows = jnp.dot(routing.astype(jnp.bfloat16), shifted, preferred_element_type=jnp.float32)
    send_rows = send_rows.astype(jnp.bfloat16).reshape(n_ori, capacity, 2 * pixel_count)
    send_class = jnp.sum(routing * classes[None, :], axis=1).reshape(n_ori, capacity)
    send_valid = jnp.sum(routing, axis=1).reshape(n_ori, capacity)
    recv_rows, recv_class, recv_valid = (
        lax.all_to_all(send_rows, "ori", split_axis=0, concat_axis=0, tiled=True),
        lax.all_to_all(send_class, "ori", split_axis=0, concat_axis=0, tiled=True),
        lax.all_to_all(send_valid, "ori", split_axis=0, concat_axis=0, tiled=True),
    )
    recv_rows = recv_rows.reshape(n_slots, 2 * pixel_count)
    recv_class = recv_class.reshape(n_slots)
    recv_valid = recv_valid.reshape(n_slots)
    scores = score_rows(recv_rows, references)
    top_score = jnp.max(scores, axis=1)
    exp_total = jnp.sum(jnp.exp(scores - top_score[:, None]), axis=1)
    peak_back, total_back = (
        lax.all_to_all(
            top_score.reshape(n_ori, capacity), "ori", split_axis=0, concat_axis=0, tiled=True
        ),
        lax.all_to_all(
            exp_total.reshape(n_ori, capacity), "ori", split_axis=0, concat_axis=0, tiled=True
        ),
    )
    peak_copy = peak_back.reshape(-1)[position].reshape(part_count, top_count)
    total_copy = total_back.reshape(-1)[position].reshape(part_count, top_count)
    evidence = combine_stats(peak_copy, total_copy)
    send_evidence = jnp.sum(routing.astype(jnp.float32) * evidence[None, :], axis=1).reshape(
        n_ori, capacity
    )
    slot_evidence = lax.all_to_all(
        send_evidence, "ori", split_axis=0, concat_axis=0, tiled=True
    ).reshape(n_slots)
    weights = jnp.exp(scores - slot_evidence[:, None]) * recv_valid.astype(jnp.float32)[:, None]
    per_ref = jnp.sum(weights.reshape(n_slots, NSHIFT, refs_dev), axis=1)
    class_picks = (recv_class[:, None] == jnp.arange(ctf_table.shape[0])[None, :]).astype(
        jnp.float32
    )
    ctf_slot = jnp.dot(class_picks, ctf_table, precision=lax.Precision.HIGHEST)
    ctf_weight = jnp.dot(per_ref.T, ctf_slot * ctf_slot, precision=lax.Precision.HIGHEST)
    light_weights = weights.astype(jnp.bfloat16).reshape(n_slots, n_blocks, shift_block * refs_dev)
    light_weights = jnp.transpose(light_weights, (1, 0, 2))

    def add_block(back_acc, inputs):
        block_id, piece_w = inputs
        gathered = jnp.dot(piece_w.T, recv_rows, preferred_element_type=jnp.float32)
        gathered = gathered.reshape(shift_block, refs_dev, 2 * pixel_count)
        cosine, sine_table = phases(*grid_shifts(block_id * shift_block, shift_block))
        g_real = gathered[..., :pixel_count]
        g_imag = gathered[..., pixel_count:]
        cos_b = cosine[:, None, :]
        sin_b = sine_table[:, None, :]
        block_sum = jnp.concatenate(
            [
                jnp.sum(cos_b * g_real + sin_b * g_imag, axis=0),
                jnp.sum(cos_b * g_imag - sin_b * g_real, axis=0),
            ],
            axis=-1,
        )
        return (back_acc + block_sum, None)

    back_acc, _ = lax.scan(
        add_block,
        jnp.zeros((refs_dev, 2 * pixel_count), jnp.float32),
        (jnp.arange(n_blocks), light_weights),
    )
    back_part, weight_part = (
        lax.psum_scatter(back_acc, "grp", scatter_dimension=1, tiled=True),
        lax.psum_scatter(ctf_weight, "grp", scatter_dimension=1, tiled=True),
    )
    return (back_part, weight_part, evidence)


def solution(mesh):
    placed = (
        P(("grp", "ori"), None),
        P(("grp", "ori"), None),
        P(None, ("grp", "ori")),
        P(("grp", "ori")),
        P(),
        P("ori", None),
    )
    return jax.shard_map(
        per_device,
        mesh=mesh,
        in_specs=placed,
        out_specs=(P("ori", "grp"), P("ori", "grp"), P(("grp", "ori"))),
        check_vma=False,
    )
```

profile of v0, /device:TPU:0, one launch (start us, length us, event | category | flops | bytes accessed | tf_op | source)
XLA Modules:
  0.0 508.2 jit_solution(328054799035579250)
XLA Ops:
  10.0 6.2 %fusion.25 = (bf16[32,8320]{1,0:T(8,128)(2,1)S(1)}, bf16[32,8320]{1,0:T(8,128)(2,1)S(1)}) fusion(f32[8320]{0:T(1024)S(1)} %mul.398, f32[32]{0:T(128)S(1)} %get-tuple-element.264, f32[8320]{0:T(1024)S(1)} %mul.394, f32[32]{0:T(128)S(1)} %get-tuple-element.263, bf16[32,16640]{1,0:T(8,128)(2,1)} %param.10, f32[16,8320]{1,0:T(8,128)S(1)} %copy-done, s32[32]{0:T(128)} %param.13), kind=kOutput, calls=%fused_computation.58 | convolution fusion | flops 55378432 | bytes 2729344 | tf_op jit(solution)/shard_map/dot_general | solution.py:81
  19.6 5.3 %all-to-all-start = ((bf16[8,16,16640]{2,1,0:T(8,128)(2,1)}), bf16[8,16,16640]{2,1,0:T(8,128)(2,1)}, u32[]{:S(2)}, u32[]{:S(2)}) async-start(bf16[8,16,16640]{2,1,0:T(8,128)(2,1)} %bitcast.70), calls=%async_computation | async-start | bytes 8519680 | tf_op jit(solution)/shard_map/all_to_all | solution.py:111
  25.8 49.0 %all-to-all-done = bf16[8,16,16640]{2,1,0:T(8,128)(2,1)} async-done(((bf16[8,16,16640]{2,1,0:T(8,128)(2,1)}), bf16[8,16,16640]{2,1,0:T(8,128)(2,1)}, u32[]{:S(2)}, u32[]{:S(2)}) %all-to-all-start) | async-done | bytes 4259872 | tf_op jit(solution)/shard_map/all_to_all | solution.py:111
  78.1 115.1 %while.27 = (s32[]{:T(128)}, f32[16,128,64]{1,2,0:T(8,128)S(1)}, s32[16]{0:T(128)S(1)}, bf16[16,16640]{1,0:T(8,128)(2,1)S(1)}, bf16[128,16640]{1,0:T(8,128)(2,1)}, /*index=5*/s32[]{:T(128)}, s32[1]{0:T(128)}) while((s32[]{:T(128)}, f32[16,128,64]{1,2,0:T(8,128)S(1)}, s32[16]{0:T(128)S(1)}, bf16[16,16640]{1,0:T(8,128)(2,1)S(1)}, ...), condition=%wide.region_4.5_spmd, body=%wide.region_3.4_spmd.sunk | while | flops 281549472 | bytes 12015293 | solution.py:61
  81.6 3.8 fusion.67
  88.8 3.8 fusion.67
  96.0 3.8 fusion.67
  110.3 3.8 fusion.67
  117.5 3.8 fusion.67
  131.9 3.8 fusion.67
  139.1 3.8 fusion.67
  146.3 3.8 fusion.67
  153.5 3.8 fusion.67
  160.7 3.8 fusion.67
  175.1 3.8 fusion.67
  182.3 3.8 fusion.67
  194.3 4.1 all-to-all-start.2
  206.4 3.9 convolution_multiply_fusion
  211.6 4.1 all-to-all-start.4
  224.0 4.2 all-to-all-done.3
  229.2 10.0 %convolution_bitcast_fusion = f32[8320,16]{1,0:T(8,128)} fusion(f32[128,16]{0,1:T(8,128)S(1)} %multiply_reduce_fusion, f32[128,8320]{1,0:T(8,128)} %convolution_multiply_fusion), kind=kOutput, calls=%fused_computation.51 | convolution fusion | flops 204472320 | bytes 4800512
  239.3 107.1 %while.28 = (s32[]{:T(128)}, f32[16,16640]{1,0:T(8,128)S(1)}, s32[16]{0:T(128)S(1)}, bf16[16,128,64]{1,2,0:T(8,128)(2,1)S(1)}, bf16[128,16640]{1,0:T(8,128)(2,1)}, /*index=5*/s32[]{:T(128)}, s32[1]{0:T(128)}, s32[]{:T(128)}) while((s32[]{:T(128)}, f32[16,16640]{1,0:T(8,128)S(1)}, s32[16]{0:T(128)S(1)}, ...), condition=%wide.region_14.15_spmd.clone, body=%wide.region_11.14_spmd.clone.sunk | while | flops 277555872 | bytes 17888976 | solution.py:166
  346.5 4.9 copy.28
  353.7 144.7 %reduce-scatter.7.cloned.1.call-done = f32[4160,16]{1,0:T(8,128)} async-done(((f32[16640,16]{1,0:T(8,128)}), f32[4160,16]{1,0:T(8,128)}) %reduce-scatter.7.cloned.1.call-update) | async-done | bytes 266256
  (464 shorter events, 189.0 us)
Async XLA Ops:
  7.2 2.8 copy-start
  19.6 5.4 %copy-start.2 = (s32[32]{0:T(128)S(1)}, s32[32]{0:T(128)}, u32[]{:S(2)}) copy-start(s32[32]{0:T(128)} %param.13) | copy-start | bytes 388
  19.6 58.5 %copy-start.1 = (bf16[16,16640]{1,0:T(8,128)(2,1)S(1)}, bf16[16,16640]{1,0:T(8,128)(2,1)}, u32[]{:S(2)}) copy-start(bf16[16,16640]{1,0:T(8,128)(2,1)} %param.15) | copy-start | bytes 1597444
  19.6 55.2 %all-to-all-start = ((bf16[8,16,16640]{2,1,0:T(8,128)(2,1)}), bf16[8,16,16640]{2,1,0:T(8,128)(2,1)}, u32[]{:S(2)}, u32[]{:S(2)}) async-start(bf16[8,16,16640]{2,1,0:T(8,128)(2,1)} %bitcast.70), calls=%async_computation | async-start | bytes 8519680 | tf_op jit(solution)/shard_map/all_to_all | solution.py:111
  74.8 119.5 %all-to-all-start.5 = ((s32[8,1,16]{2,1,0:T(1,128)}), s32[8,1,16]{2,1,0:T(1,128)S(1)}, u32[]{:S(2)}, u32[]{:S(2)}) async-start(s32[8,1,16]{2,1,0:T(1,128)} %bitcast.17), calls=%async_computation.5 | async-start | bytes 8192 | tf_op jit(solution)/shard_map/all_to_all | solution.py:112
  194.3 8.8 %all-to-all-start.2 = ((f32[8,1,16]{2,1,0:T(1,128)}), f32[8,1,16]{2,1,0:T(1,128)S(1)}, u32[]{:S(2)}, u32[]{:S(2)}) async-start(f32[8,1,16]{2,1,0:T(1,128)} %bitcast.12), calls=%async_computation.2 | async-start | bytes 8192 | tf_op jit(solution)/shard_map/all_to_all | solution.py:125
  203.1 8.5 %all-to-all-start.1 = ((f32[8,1,16]{2,1,0:T(1,128)}), f32[8,1,16]{2,1,0:T(1,128)S(1)}, u32[]{:S(2)}, u32[]{:S(2)}) async-start(f32[8,1,16]{2,1,0:T(1,128)} %bitcast.9), calls=%async_computation.1 | async-start | bytes 8192 | tf_op jit(solution)/shard_map/all_to_all | solution.py:122
  211.6 8.8 %all-to-all-start.4 = ((s32[8,1,16]{2,1,0:T(1,128)}), s32[8,1,16]{2,1,0:T(1,128)S(1)}, u32[]{:S(2)}, u32[]{:S(2)}) async-start(s32[8,1,16]{2,1,0:T(1,128)} %bitcast.14), calls=%async_computation.4 | async-start | bytes 8192 | tf_op jit(solution)/shard_map/all_to_all | solution.py:113
  218.6 20.7 %copy-start.3 = (f32[32]{0:T(128)}, f32[32]{0:T(128)S(1)}, u32[]{:S(2)}) copy-start(f32[32]{0:T(128)S(1)} %log_add_fusion) | copy-start | bytes 388
  220.4 7.9 %all-to-all-start.3 = ((f32[8,1,16]{2,1,0:T(1,128)}), f32[8,1,16]{2,1,0:T(1,128)S(1)}, u32[]{:S(2)}, u32[]{:S(2)}) async-start(f32[8,1,16]{2,1,0:T(1,128)} %bitcast.13), calls=%async_computation.3 | async-start | bytes 8192 | tf_op jit(solution)/shard_map/all_to_all | solution.py:135
  223.7 127.8 %reduce-scatter.9.cloned.1.call-start = ((), (), s32[]{:S(2)}) async-start(), calls=%async_computation.9 | async-start | bytes 5324800
  239.3 259.1 %reduce-scatter.7.cloned.1.call-start = ((), (), s32[]{:S(2)}) async-start(), calls=%async_computation.8 | async-start | bytes 10649600
Sparse Core Ops, SparseCore 0:
  239.4 77.9 reduce-scatter.8
  351.5 146.8 reduce-scatter.6
where the time goes:
time: 510 us; the launch traced here: 508 us
  waiting for transfers between devices  201 us (39%)
  matrix products  130 us (25%)
  other arithmetic  62.3 us (12%)
  local copies, waits for them, and re-layouts  53.1 us (10%)
  starting transfers between devices  23.8 us (5%)
  loops' own time  23.3 us (5%)
  between operations  14.3 us (3%)
    unnamed x4, waiting for transfers between devices  145 us
    dot_general x16, matrix products, one_block(): return jnp.dot(slot_rows, kernel_rows.T, preferred_element_type=jnp.float32)  60 us
    all_to_all x1, waiting for transfers between devices, per_device(): lax.all_to_all(send_rows, 'ori', split_axis=0, concat_axis=0, tiled=True)  49 us
    dot_general x16, matrix products, add_block(): gathered = jnp.dot(piece_w.T, recv_rows, preferred_element_type=jnp.float32)  46.9 us
    cos x32, other arithmetic, phases(): return (jnp.cos(angle_grid), jnp.sin(angle_grid))  32.9 us
    dynamic_slice x32, local copies, waits for them, and re-layouts, score_rows(): stacked = lax.map(one_block, jnp.arange(n_blocks))  18.9 us
    another operation x1, loops' own time, per_device(): lax.scan(add_block, jnp.zeros((refs_dev, 2 * pixel_count), jnp.float32),...  11.7 us
    another operation x1, loops' own time, score_rows(): stacked = lax.map(one_block, jnp.arange(n_blocks))  11.6 us
  transfers between devices with their start and end apart: 8, of which 5 were waited for; matrix products, arithmetic and copies ran while one was open for 43% of the time, Pallas kernels for 0%

commit v1 on v0

v1 whole, which is shorter than its diff:
```python
import functools
import math

import jax
import jax.numpy as jnp
from jax import lax
from jax.experimental import pallas as pl
from jax.experimental.pallas import tpu as pltpu
from jax.sharding import PartitionSpec as P

PX = 128
PY = 65
BOX = 320
SIDE = 8
NSHIFT = 64
HALF = NSHIFT // 2
LANES = 128

two_pi = 2.0 * math.pi
pixel_count = PX * PY
steps = 5
chunk = pixel_count // steps


def frequencies():
    pixel = jnp.arange(pixel_count)
    row_ids = pixel // PY
    freq_x = jnp.where(row_ids < PX // 2, row_ids, row_ids - PX).astype(jnp.float32)
    freq_y = (pixel % PY).astype(jnp.float32)
    return freq_x, freq_y


def axis_table(freq, amounts):
    angle = two_pi * (amounts[:, None] * freq[None, :]) / BOX
    return jnp.cos(angle), jnp.sin(angle)


def outer_table(table_x, table_y):
    cx, sx = table_x
    cy, sy = table_y
    cosine = cx[:, None] * cy[None] - sx[:, None] * sy[None]
    sine = sx[:, None] * cy[None] + cx[:, None] * sy[None]
    count = cx.shape[0] * cy.shape[0]
    return cosine.reshape(count, -1), sine.reshape(count, -1)


def pick(table, ids):
    out = jnp.zeros((ids.shape[0], table.shape[1]), jnp.float32)
    for i in range(table.shape[0]):
        out = jnp.where(ids[:, None] == i, table[i][None, :], out)
    return out


def centered(particles, offsets, classes, ctf_table, freq_x, freq_y):
    class_picks = (classes[:, None] == jnp.arange(ctf_table.shape[0])[None, :]).astype(jnp.float32)
    ctf_rows = jnp.dot(class_picks, ctf_table, precision=lax.Precision.HIGHEST)
    amounts = jnp.arange(-2, 3).astype(jnp.float32)
    cx, sx = axis_table(freq_x, amounts)
    cy, sy = axis_table(freq_y, amounts)
    ox, oy = offsets[0] + 2, offsets[1] + 2
    cx, sx, cy, sy = pick(cx, ox), pick(sx, ox), pick(cy, oy), pick(sy, oy)
    cosine = cx * cy - sx * sy
    sine = sx * cy + cx * sy
    real_part = particles[:, :pixel_count].astype(jnp.float32)
    imag_part = particles[:, pixel_count:].astype(jnp.float32)
    return jnp.concatenate(
        [
            ctf_rows * (real_part * cosine + imag_part * sine),
            ctf_rows * (imag_part * cosine - real_part * sine),
        ],
        axis=-1,
    ).astype(jnp.bfloat16)


def score_kernel(rr_ref, ri_ref, mr_ref, mi_ref, cos_ref, sin_ref, out_ref, lse_ref, kern):
    step = pl.program_id(0)
    refs = mr_ref.shape[0]

    def lane_block(j, carry):
        lanes = pl.ds(pl.multiple_of(j * LANES, LANES), LANES)
        late = pl.ds(pl.multiple_of(chunk + j * LANES, LANES), LANES)
        re = mr_ref[:, lanes].astype(jnp.float32)
        im = mi_ref[:, lanes].astype(jnp.float32)
        for s in range(NSHIFT):
            c = cos_ref[s : s + 1, lanes]
            d = sin_ref[s : s + 1, lanes]
            kern[s * refs : (s + 1) * refs, lanes] = (c * re - d * im).astype(jnp.bfloat16)
            kern[s * refs : (s + 1) * refs, late] = (d * re + c * im).astype(jnp.bfloat16)
        return carry

    lax.fori_loop(0, chunk // LANES, lane_block, 0)

    @pl.when(step == 0)
    def _():
        out_ref[...] = jnp.zeros_like(out_ref)

    tile = 256

    def row_block(j, carry):
        rows = pl.ds(pl.multiple_of(j * tile, tile), tile)
        dims = (((1,), (1,)), ((), ()))
        part = lax.dot_general(
            kern[rows, :chunk], rr_ref[...], dims, preferred_element_type=jnp.float32
        )
        part += lax.dot_general(
            kern[rows, chunk:], ri_ref[...], dims, preferred_element_type=jnp.float32
        )
        out_ref[rows, :] += part
        return carry

    lax.fori_loop(0, NSHIFT * refs // tile, row_block, 0)

    @pl.when(step == steps - 1)
    def _():
        scores = out_ref[...] * (2.0 / math.sqrt(pixel_count))
        out_ref[...] = scores
        top = jnp.max(scores, axis=0, keepdims=True)
        total = jnp.sum(jnp.exp(scores - top), axis=0, keepdims=True)
        lse_ref[...] = top + jnp.log(total)


def score_call(rows, references, cosine, sine):
    n_rows, refs = rows.shape[0], references.shape[0]
    hyps = NSHIFT * refs
    return pl.pallas_call(
        score_kernel,
        grid=(steps,),
        in_specs=[
            pl.BlockSpec((n_rows, chunk), lambda i: (0, i)),
            pl.BlockSpec((n_rows, chunk), lambda i: (0, i + steps)),
            pl.BlockSpec((refs, chunk), lambda i: (0, i)),
            pl.BlockSpec((refs, chunk), lambda i: (0, i + steps)),
            pl.BlockSpec((NSHIFT, chunk), lambda i: (0, i)),
            pl.BlockSpec((NSHIFT, chunk), lambda i: (0, i)),
        ],
        out_specs=[
            pl.BlockSpec((hyps, n_rows), lambda i: (0, 0)),
            pl.BlockSpec((1, n_rows), lambda i: (0, 0)),
        ],
        out_shape=[
            jax.ShapeDtypeStruct((hyps, n_rows), jnp.float32),
            jax.ShapeDtypeStruct((1, n_rows), jnp.float32),
        ],
        scratch_shapes=[pltpu.VMEM((hyps, 2 * chunk), jnp.bfloat16)],
        compiler_params=pltpu.CompilerParams(vmem_limit_bytes=60 * 2**20),
    )(rows, rows, references, references, cosine, sine)


def back_kernel(wp_ref, wm_ref, rr_ref, ri_ref, cos_ref, sin_ref, hc_ref, hs_ref, re_ref, im_ref):
    refs = re_ref.shape[0]

    def lane_block(j, carry):
        lanes = pl.ds(pl.multiple_of(j * LANES, LANES), LANES)
        panel = jnp.concatenate([rr_ref[:, lanes], ri_ref[:, lanes]], axis=1)
        even = jnp.dot(wp_ref[...], panel, preferred_element_type=jnp.float32)
        odd = jnp.dot(wm_ref[...], panel, preferred_element_type=jnp.float32)
        re = jnp.zeros((refs, LANES), jnp.float32)
        im = jnp.zeros((refs, LANES), jnp.float32)
        for s in range(HALF):
            c = cos_ref[s : s + 1, lanes]
            d = sin_ref[s : s + 1, lanes]
            e = even[s * refs : (s + 1) * refs]
            o = odd[s * refs : (s + 1) * refs]
            re += c * e[:, :LANES] + d * o[:, LANES:]
            im += c * e[:, LANES:] - d * o[:, :LANES]
        hc = hc_ref[:, lanes]
        hs = hs_ref[:, lanes]
        re_ref[:, lanes] = hc * re - hs * im
        im_ref[:, lanes] = hc * im + hs * re
        return carry

    lax.fori_loop(0, chunk // LANES, lane_block, 0)


def back_call(w_even, w_odd, rows, cosine, sine, half_cos, half_sin, refs):
    n_rows = rows.shape[0]
    whole = pl.BlockSpec(w_even.shape, lambda i: (0, 0))
    part = lambda count: pl.BlockSpec((count, chunk), lambda i: (0, i))
    return pl.pallas_call(
        back_kernel,
        grid=(steps,),
        in_specs=[
            whole,
            whole,
            part(n_rows),
            pl.BlockSpec((n_rows, chunk), lambda i: (0, i + steps)),
            part(HALF),
            part(HALF),
            part(1),
            part(1),
        ],
        out_specs=[part(refs), part(refs)],
        out_shape=[jax.ShapeDtypeStruct((refs, pixel_count), jnp.float32)] * 2,
        compiler_params=pltpu.CompilerParams(vmem_limit_bytes=60 * 2**20),
        cost_estimate=pl.CostEstimate(
            flops=4 * HALF * refs * n_rows * 2 * pixel_count,
            bytes_accessed=4 * n_rows * pixel_count,
            transcendentals=0,
        ),
    )(w_even, w_odd, rows, rows, cosine, sine, half_cos, half_sin)


def per_device(particles, priors, offsets, classes, ctf_table, references):
    n_ori = lax.axis_size("ori")
    n_grp = lax.axis_size("grp")
    me = lax.axis_index("ori")
    part_count = priors.shape[0]
    refs = references.shape[0]
    n_classes = ctf_table.shape[0]
    freq_x, freq_y = frequencies()
    shifted = centered(particles, offsets, classes, ctf_table, freq_x, freq_y)
    rows = lax.all_gather(shifted, "ori", axis=0, tiled=True)
    facts = lax.all_gather(
        jnp.concatenate([priors, classes[:, None]], axis=1).T, "ori", axis=1, tiled=True
    )
    first, second, row_class = facts[0], facts[1], facts[2]

    whole_steps = jnp.arange(SIDE).astype(jnp.float32) - SIDE // 2
    cosine, sine = outer_table(axis_table(freq_x, whole_steps), axis_table(freq_y, whole_steps))
    near = whole_steps + 0.5
    near_cos, near_sin = outer_table(
        axis_table(freq_x, near[: SIDE // 2]), axis_table(freq_y, near)
    )
    half_angle = (0.5 * two_pi / BOX) * (freq_x + freq_y)[None, :]
    half_cos, half_sin = jnp.cos(half_angle), jnp.sin(half_angle)

    scores, lse = score_call(rows, references, cosine, sine)
    all_lse = lax.all_gather(lse[0], "ori", axis=0, tiled=False)
    owners = jnp.arange(n_ori)[:, None]
    named = (first[None, :] == owners) | (second[None, :] == owners)
    kept = jnp.where(named, all_lse, -jnp.inf)
    top = jnp.max(kept, axis=0)
    evidence = top + jnp.log(jnp.sum(jnp.exp(kept - top[None, :]), axis=0))

    mine = (first == me) | (second == me)
    weights = jnp.where(mine[None, :], jnp.exp(scores - evidence[None, :]), 0.0)
    weights = weights.reshape(NSHIFT, refs, -1)
    per_ref = jnp.sum(weights, axis=0)
    ahead = weights[:HALF]
    behind = weights[HALF:][::-1]
    w_even = (ahead + behind).astype(jnp.bfloat16).reshape(HALF * refs, -1)
    w_odd = (ahead - behind).astype(jnp.bfloat16).reshape(HALF * refs, -1)

    class_picks = (row_class[:, None] == jnp.arange(n_classes)[None, :]).astype(jnp.float32)
    by_class = jnp.dot(per_ref, class_picks, precision=lax.Precision.HIGHEST)
    by_class = lax.psum(by_class, "grp")
    width = pixel_count // n_grp
    table_part = lax.dynamic_slice_in_dim(ctf_table, lax.axis_index("grp") * width, width, 1)
    weight_part = jnp.dot(by_class, table_part * table_part, precision=lax.Precision.HIGHEST)

    back_re, back_im = back_call(
        w_even, w_odd, rows, near_cos, near_sin, half_cos, half_sin, refs
    )
    pieces = [
        jnp.transpose(x.reshape(refs, n_grp // 2, -1), (1, 0, 2)) for x in (back_re, back_im)
    ]
    back_part = lax.psum_scatter(
        jnp.concatenate(pieces, axis=0), "grp", scatter_dimension=0, tiled=False
    )
    own = lax.dynamic_slice_in_dim(evidence, me * part_count, part_count, 0)
    return (back_part, weight_part, own)


def solution(mesh):
    placed = (
        P(("grp", "ori"), None),
        P(("grp", "ori"), None),
        P(None, ("grp", "ori")),
        P(("grp", "ori")),
        P(),
        P("ori", None),
    )
    return jax.shard_map(
        per_device,
        mesh=mesh,
        in_specs=placed,
        out_specs=(P("ori", "grp"), P("ori", "grp"), P(("grp", "ori"))),
        check_vma=False,
    )
```

time: 510 us -> 174 us (0.34)
  waiting for transfers between devices: 201 us -> 50.8 us
  matrix products: 130 us -> 3.65 us
  Pallas kernels: 0 us -> 48.8 us
  local copies, waits for them, and re-layouts: 53.1 us -> 5.14 us
  other arithmetic: 62.3 us -> 19 us
  blocking collectives: 0 us -> 31.7 us
  starting transfers between devices: 23.8 us -> 0.08 us
  loops' own time: 23.3 us -> 0 us
    unnamed x4 -> x2, waiting for transfers between devices: 145 us -> 0.03 us
    dot_general x34 -> x2, matrix products: 114 us -> 1.22 us  [the longest x1 0.99 us: per_device(): jnp.dot(by_class, table_part * table_part, precision=lax.Precision.HIGHEST)]
    all_to_all x6 -> x0, waiting for transfers between devices: 56.3 us -> none  [the longest x1 49 us: per_device(): lax.all_to_all(send_rows, 'ori', split_axis=0, concat_axis=0, tiled=True)]
    pallas_call x0 -> x2, Pallas kernels: none -> 48.8 us  [the longest x1 26 us: score_call(): pl.pallas_call(score_kernel, grid=(steps,), in_specs=[pl.BlockSpec((n_row...]
    all_gather x0 -> x1, waiting for transfers between devices: none -> 36.8 us  [per_device(): rows = lax.all_gather(shifted, 'ori', axis=0, tiled=True)]
    cos x32 -> x3, other arithmetic: 32.9 us -> 5.8 us  [axis_table(): return (jnp.cos(angle), jnp.sin(angle))]
    all_to_all x6 -> x0, starting transfers between devices: 23.5 us -> none  [the longest x1 5.32 us: per_device(): lax.all_to_all(send_rows, 'ori', split_axis=0, concat_axis=0, tiled=True)]
    another operation x2 -> x0, loops' own time: 23.3 us -> none  [the longest x1 11.7 us: per_device(): lax.scan(add_block, jnp.zeros((refs_dev, 2 * pixel_count), jnp.float32),...]
  transfers between devices with their start and end apart: 8 -> 2, of which waited for: 5 -> 2; matrix products, arithmetic and copies ran while one was open for 43% -> 7% of each run, Pallas kernels for 0% -> 0%
where the time goes in v1:
time: 174 us; the launch traced here: 173 us
  waiting for transfers between devices  50.8 us (29%)
  Pallas kernels  48.8 us (28%)
  blocking collectives  31.7 us (18%)
  other arithmetic  19 us (11%)
  between operations  14.2 us (8%)
  local copies, waits for them, and re-layouts  5.14 us (3%)
  matrix products  3.65 us (2%)
    all_gather x1, waiting for transfers between devices, per_device(): rows = lax.all_gather(shifted, 'ori', axis=0, tiled=True)  36.8 us
    pallas_call x1, Pallas kernels, score_call(): pl.pallas_call(score_kernel, grid=(steps,), in_specs=[pl.BlockSpec((n_row...  26 us
    pallas_call x1, Pallas kernels, back_call(): pl.pallas_call(back_kernel, grid=(steps,), in_specs=[whole, whole, part(n...  22.8 us
    reduce_scatter x1, waiting for transfers between devices, per_device(): lax.psum_scatter(jnp.concatenate(pieces, axis=0), 'grp', scatter_dimensio...  14 us
    psum x1, blocking collectives, per_device(): by_class = lax.psum(by_class, 'grp')  12.3 us
    all_gather x1, blocking collectives, per_device(): lax.all_gather(jnp.concatenate([priors, classes[:, None]], axis=1).T, 'or...  10.6 us
    all_gather x1, blocking collectives, per_device(): all_lse = lax.all_gather(lse[0], 'ori', axis=0, tiled=False)  8.87 us
    cos x3, other arithmetic, axis_table(): return (jnp.cos(angle), jnp.sin(angle))  5.8 us
  transfers between devices with their start and end apart: 2, of which 2 were waited for; matrix products, arithmetic and copies ran while one was open for 7% of the time, Pallas kernels for 0%

profile of v1, /device:TPU:0, one launch (start us, length us, event | category | flops | bytes accessed | tf_op | source)
XLA Modules:
  0.0 173.4 jit_solution(3870582682791455559)
XLA Ops:
  7.3 0.8 compare_bitcast_fusion.9
  8.1 1.9 %fusion.15 = (f32[5,8320]{1,0:T(8,128)S(1)}, f32[5,8320]{1,0:T(8,128)S(1)}, f32[5,8320]{1,0:T(8,128)S(1)}, f32[5,8320]{1,0:T(8,128)S(1)}) fusion(f32[8320]{0:T(1024)S(1)} %fusion.29, f32[5]{0:T(128)S(1)} %add_convert_fusion.1, f32[8320]{0:T(1024)S(1)} %fusion.30), kind=kLoop, calls=%fused_computation.41 | loop fusion | flops 166400 | bytes 732180 | tf_op jit(solution)/shard_map/cos | solution.py:35
  10.0 0.9 slice_reduce_fusion.14
  10.9 0.9 slice_reduce_fusion.4
  11.8 2.4 %fusion.5 = (bf16[32,8320]{1,0:T(8,128)(2,1)S(1)}, f32[32,8320]{1,0:T(8,128)S(1)}) fusion(bf16[32,16640]{1,0:T(8,128)(2,1)S(1)} %copy-done, f32[8320]{0:T(1024)S(1)} %get-tuple-element.27, f32[8320]{0:T(1024)S(1)} %get-tuple-element.28, f32[8320]{0:T(1024)S(1)} %get-tuple-element.29, f32[8320]{0:T(1024)S(1)} %get-tuple-element.30, ...), kind=kOutput, calls=%fused_computation.12 | convolution fusion | flops 59904512 | bytes 3860928 | tf_op jit(solution)/shard_map/dot_general | solution.py:56
  14.3 2.1 %fusion.2 = bf16[32,8320]{1,0:T(8,128)(2,1)S(1)} fusion(f32[32,8320]{1,0:T(8,128)S(1)} %get-tuple-element.71, bf16[32,16640]{1,0:T(8,128)(2,1)S(1)} %copy-done, f32[8320]{0:T(1024)S(1)} %get-tuple-element.27, f32[8320]{0:T(1024)S(1)} %get-tuple-element.28, f32[8320]{0:T(1024)S(1)} %get-tuple-element.29, f32[8320]{0:T(1024)S(1)} %get-tuple-element.30, ...), kind=kLoop, calls=%fused_computation.9 | loop fusion | flops 8785920 | bytes 3328320 | tf_op jit(solution)/shard_map/convert
  16.4 1.1 pad_maximum_fusion.1
  18.1 10.6 %all-gather = s32[8,32,3]{1,2,0:T(4,128)S(1)} all-gather(s32[1,32,3]{1,2,0:T(4,128)S(1)} %add_bitcast_fusion.2), channel_id=1, replica_groups=mesh['grp'=4,'ori'=8] {'ori'}, dimensions={0}, use_global_device_ids=true | all-gather | bytes 3456 | tf_op jit(solution)/shard_map/all_gather | solution.py:213
  28.8 1.7 fusion.36
  30.5 1.0 fusion.20
  31.5 2.9 %fusion.7 = (f32[8,8320]{1,0:T(8,128)S(1)}, f32[8,8320]{1,0:T(8,128)S(1)}, f32[8,8320]{1,0:T(8,128)S(1)}, f32[8,8320]{1,0:T(8,128)S(1)}, f32[8,8320]{1,0:T(8,128)S(1)}, /*index=5*/f32[8,8320]{1,0:T(8,128)S(1)}) fusion(f32[8]{0:T(128)S(1)} %get-tuple-element.82, f32[8320]{0:T(1024)S(1)} %fusion.30, f32[8]{0:T(128)S(1)} %get-tuple-element.83, f32[8320]{0:T(1024)S(1)} %fusion.29), kind=kLoop, calls=%fused_computation.29 | loop fusion | flops 399360 | bytes 1664064 | tf_op jit(solution)/shard_map/cos | solution.py:35
  34.4 1.6 add_bitcast_fusion.1
  36.0 2.4 %add_bitcast_fusion = (f32[64,8320]{1,0:T(8,128)}, f32[64,8320]{1,0:T(8,128)}) fusion(f32[8,8320]{1,0:T(8,128)S(1)} %get-tuple-element.51, f32[8,8320]{1,0:T(8,128)S(1)} %get-tuple-element.66, f32[8,8320]{1,0:T(8,128)S(1)} %get-tuple-element.52, f32[8,8320]{1,0:T(8,128)S(1)} %get-tuple-element.67), kind=kLoop, calls=%fused_computation | loop fusion | flops 3194880 | bytes 5324800 | tf_op jit(solution)/shard_map/add | solution.py:42
  38.4 36.8 %all-gather.4.cloned.1.call-done.rr_ref.ri_ref = bf16[256,16640]{1,0:T(8,128)(2,1)} async-done(((bf16[32,16640]{1,0:T(8,128)(2,1)}), bf16[256,16640]{1,0:T(8,128)(2,1)}) %all-gather.4.cloned.1.call-update) | async-done | bytes 8519696 | tf_op jit(solution)/shard_map/all_gather | solution.py:212
  75.1 26.0 %shard_map.85 = (f32[1024,256]{1,0:T(8,128)}, f32[1,256]{1,0:T(1,128)}) custom-call(bf16[256,16640]{1,0:T(8,128)(2,1)} %all-gather.4.cloned.1.call-done.rr_ref.ri_ref, bf16[256,16640]{1,0:T(8,128)(2,1)} %all-gather.4.cloned.1.call-done.rr_ref.ri_ref, bf16[16,16640]{1,0:T(8,128)(2,1)} %mi_ref.1, bf16[16,16640]{1,0:T(8,128)(2,1)} %mi_ref.1, ...), custom_call_target="tpu_custom_call" | custom-call | tf_op jit(solution)/shard_map/pallas_call | solution.py:125
  101.1 8.9 %all-gather.1 = f32[8,1,256]{2,1,0:T(1,128)S(1)} all-gather(f32[1,1,256]{2,1,0:T(1,128)} %bitcast.74), channel_id=1, replica_groups=mesh['grp'=4,'ori'=8] {'ori'}, dimensions={0}, use_global_device_ids=true | all-gather | bytes 9216 | tf_op jit(solution)/shard_map/all_gather | solution.py:228
  110.0 1.4 exponential_select_fusion
  111.5 0.9 subtract_convert_fusion
  112.4 22.8 %shard_map.86 = (f32[16,8320]{1,0:T(8,128)}, f32[16,8320]{1,0:T(8,128)}) custom-call(bf16[512,256]{1,0:T(8,128)(2,1)} %bitcast.66, bf16[512,256]{1,0:T(8,128)(2,1)} %bitcast.65, bf16[256,16640]{1,0:T(8,128)(2,1)} %all-gather.4.cloned.1.call-done.rr_ref.ri_ref, bf16[256,16640]{1,0:T(8,128)(2,1)} %all-gather.4.cloned.1.call-done.rr_ref.ri_ref, ...), custom_call_target="tpu_custom_call" | custom-call | flops 8724152320 | bytes 8519680 | tf_op jit(solution)/shard_map/pallas_call | solution.py:179
  135.2 1.5 reshape.445
  137.3 1.1 pad_maximum_fusion
  139.3 12.3 %psum.7 = f32[16,16]{1,0:T(8,128)S(1)} all-reduce(f32[16,16]{1,0:T(8,128)S(1)} %fusion.21), channel_id=1, replica_groups=mesh['grp'=4,'ori'=8] {'grp'}, use_global_device_ids=true, to_apply=%region_4.5 | all-reduce | flops 256 | bytes 2048 | tf_op jit(solution)/shard_map/psum | solution.py:246
  151.6 1.0 fusion.16
  152.6 14.0 %reduce-scatter.2.cloned.1.call-done = f32[1,16,4160]{2,1,0:T(8,128)} async-done(((f32[4,16,4160]{2,1,0:T(8,128)}), f32[1,16,4160]{2,1,0:T(8,128)}) %reduce-scatter.2.cloned.1.call-update) | async-done | bytes 266256 | tf_op jit(solution)/shard_map/reduce_scatter | solution.py:257
  (33 shorter events, 2.4 us)
Async XLA Ops:
  7.2 68.0 %all-gather.4.cloned.1.call-start = ((), (), s32[]{:S(2)}) async-start(), calls=%async_computation.1 | async-start | bytes 9584640 | tf_op jit(solution)/shard_map/all_gather | solution.py:212
  8.0 3.8 %copy-start = (bf16[32,16640]{1,0:T(8,128)(2,1)S(1)}, bf16[32,16640]{1,0:T(8,128)(2,1)}, u32[]{:S(2)}) copy-start(bf16[32,16640]{1,0:T(8,128)(2,1)} %param.6) | copy-start | bytes 3194884
  8.1 3.8 %copy-start.2 = (f32[16,8320]{1,0:T(8,128)S(1)}, f32[16,8320]{1,0:T(8,128)}, u32[]{:S(2)}) copy-start(f32[16,8320]{1,0:T(8,128)} %param.10) | copy-start | bytes 1597444
  8.1 3.8 %copy-start.4 = (s32[32]{0:T(128)S(1)}, s32[32]{0:T(128)}, u32[]{:S(2)}) copy-start(s32[32]{0:T(128)} %param.9) | copy-start | bytes 388
  17.4 0.7 copy-start.3
  17.4 149.1 %reduce-scatter.2.cloned.1.call-start = ((), (), s32[]{:S(2)}) async-start(), calls=%async_computation.2 | async-start | bytes 1351680 | tf_op jit(solution)/shard_map/reduce_scatter | solution.py:257
  135.2 1.6 copy-start.1
Sparse Core Ops, SparseCore 0:
  17.6 57.5 all-gather.3
  138.5 28.0 reduce-scatter.1

commit v2 on v1

--- a/solution.py
+++ b/solution.py
@@ -200,7 +200,7 @@
     )(w_even, w_odd, rows, rows, cosine, sine, half_cos, half_sin)
 
 
-def per_device(particles, priors, offsets, classes, ctf_table, references):
+def per_device_plain(particles, priors, offsets, classes, ctf_table, references):
     n_ori = lax.axis_size("ori")
     n_grp = lax.axis_size("grp")
     me = lax.axis_index("ori")
@@ -261,7 +261,493 @@
     return (back_part, weight_part, own)
 
 
+N_CHUNK = 13
+CHUNK_PX = pixel_count // N_CHUNK
+CHUNK_BLOCKS = CHUNK_PX // LANES
+PIECES = 11
+PIECE_BLOCKS = 3
+MESH = pl.DeviceIdType.MESH
+
+
+def square(z):
+    c, s = z
+    return c * c - s * s, 2.0 * c * s
+
+
+def times(z, y):
+    return z[0] * y[0] - z[1] * y[1], z[0] * y[1] + z[1] * y[0]
+
+
+def step_table(half):
+    one = square(half)
+    two = square(one)
+    four = square(two)
+    k = lax.broadcasted_iota(jnp.int32, (SIDE, LANES), 0)
+    out = (jnp.broadcast_to(four[0], (SIDE, LANES)), jnp.broadcast_to(-four[1], (SIDE, LANES)))
+    for bit, z in ((1, one), (2, two), (4, four)):
+        on = (k // bit) % 2 == 1
+        out = times(out, (jnp.where(on, z[0], 1.0), jnp.where(on, z[1], 0.0)))
+    return out
+
+
+def offset_phase(half, ids):
+    one = square(half)
+    two = square(one)
+    size = jnp.abs(ids)
+    c = jnp.where(size == 0, 1.0, jnp.where(size == 1, one[0], two[0]))
+    s = jnp.where(size == 0, 0.0, jnp.where(size == 1, one[1], two[1]))
+    return c, jnp.where(ids < 0, -s, s)
+
+
+def fused_kernel(
+    n_ori,
+    n_grp,
+    prt,
+    info,
+    facts,
+    base,
+    ctf,
+    mref,
+    back_out,
+    class_out,
+    ev_out,
+    rows,
+    kern,
+    scores,
+    wp,
+    wm,
+    tab_c,
+    tab_s,
+    fbuf,
+    lbuf,
+    cbuf,
+    part,
+    rbuf,
+    row_send,
+    row_recv,
+    f_send,
+    f_recv,
+    l_send,
+    l_recv,
+    c_send,
+    c_recv,
+    b_send,
+    b_recv,
+):
+    g = lax.axis_index("grp")
+    me = lax.axis_index("ori")
+    per = prt.shape[0]
+    refs = mref.shape[0]
+    core = lax.rem(me, 2)
+    px = lax.rem(me // 2, 2)
+    py = me // 4
+    dx = 2 * (1 - 2 * px)
+    dy = 4 * (1 - 2 * py)
+    sib = me + 1 - 2 * core
+    xn, yn, diag = me + dx, me + dy, me + dx + dy
+
+    barrier = pltpu.get_barrier_semaphore()
+    for k in range(1, n_ori):
+        pl.semaphore_signal(
+            barrier, inc=1, device_id=(g, lax.rem(me + k, n_ori)), device_id_type=MESH
+        )
+    for k in range(1, n_grp):
+        pl.semaphore_signal(
+            barrier, inc=1, device_id=(lax.rem(g + k, n_grp), me), device_id_type=MESH
+        )
+
+    def halves(lanes):
+        return (
+            (base[0:1, lanes], base[1:2, lanes]),
+            (base[2:3, lanes], base[3:4, lanes]),
+        )
+
+    cls = info[:, 0:1]
+    ox = info[:, 1:2]
+    oy = info[:, 2:3]
+
+    def center_block(j, carry):
+        c = j // CHUNK_BLOCKS
+        off = lax.rem(j, CHUNK_BLOCKS) * LANES
+        lanes = pl.ds(pl.multiple_of(j * LANES, LANES), LANES)
+        late = pl.ds(pl.multiple_of(pixel_count + j * LANES, LANES), LANES)
+        hx, hy = halves(lanes)
+        cosine, sine = times(offset_phase(hx, ox), offset_phase(hy, oy))
+        amp = jnp.zeros((per, LANES), jnp.float32)
+        for i in range(ctf.shape[0]):
+            amp = jnp.where(cls == i, ctf[i : i + 1, lanes], amp)
+        re = prt[:, lanes].astype(jnp.float32)
+        im = prt[:, late].astype(jnp.float32)
+        mine = pl.ds(pl.multiple_of(me * per, per), per)
+        rows[c, mine, pl.ds(pl.multiple_of(off, LANES), LANES)] = (
+            amp * (re * cosine + im * sine)
+        ).astype(jnp.bfloat16)
+        rows[c, mine, pl.ds(pl.multiple_of(CHUNK_PX + off, LANES), LANES)] = (
+            amp * (im * cosine - re * sine)
+        ).astype(jnp.bfloat16)
+        return carry
+
+    lax.fori_loop(0, N_CHUNK * CHUNK_BLOCKS, center_block, 0)
+
+    pl.semaphore_wait(barrier, n_ori - 1 + n_grp - 1)
+
+    half_rows = per // 2
+    plan = (
+        (me, 0, per, xn),
+        (me, 0, per, yn),
+        (me, 0, per, sib),
+        (xn, 0, half_rows, yn),
+        (yn, half_rows, half_rows, xn),
+        (xn, 0, per, sib),
+        (yn, 0, per, sib),
+        (diag, 0, half_rows, sib),
+        (diag, half_rows, half_rows, sib),
+    )
+
+    def row_copy(kind, c):
+        owner, first, count, target = plan[kind]
+        piece = rows.at[c, pl.ds(pl.multiple_of(owner * per + first, half_rows), count)]
+        return pltpu.make_async_remote_copy(
+            src_ref=piece,
+            dst_ref=piece,
+            send_sem=row_send.at[kind, c],
+            recv_sem=row_recv.at[kind, c],
+            device_id=(g, target),
+            device_id_type=MESH,
+        )
+
+    def fact_copy(k):
+        return pltpu.make_async_remote_copy(
+            src_ref=facts,
+            dst_ref=fbuf.at[k],
+            send_sem=f_send.at[k],
+            recv_sem=f_recv.at[k],
+            device_id=(g, lax.rem(me + k, n_ori)),
+            device_id_type=MESH,
+        )
+
+    def lse_copy(k):
+        return pltpu.make_async_remote_copy(
+            src_ref=lbuf.at[me],
+            dst_ref=lbuf.at[me],
+            send_sem=l_send.at[k],
+            recv_sem=l_recv.at[k],
+            device_id=(g, lax.rem(me + k, n_ori)),
+            device_id_type=MESH,
+        )
+
+    def class_copy(k):
+        return pltpu.make_async_remote_copy(
+            src_ref=cbuf.at[0],
+            dst_ref=cbuf.at[k],
+            send_sem=c_send.at[k],
+            recv_sem=c_recv.at[k],
+            device_id=(lax.rem(g + k, n_grp), me),
+            device_id_type=MESH,
+        )
+
+    def back_copy(k, i):
+        to = lax.rem(g + k, n_grp)
+        return pltpu.make_async_remote_copy(
+            src_ref=part.at[i, to],
+            dst_ref=rbuf.at[k, i],
+            send_sem=b_send.at[k, i],
+            recv_sem=b_recv.at[k, i],
+            device_id=(to, me),
+            device_id_type=MESH,
+        )
+
+    for c in range(2):
+        for kind in range(3):
+            row_copy(kind, c).start()
+    for k in range(1, n_ori):
+        fact_copy(k).start()
+
+    scores[...] = jnp.zeros_like(scores)
+
+    def make_kernels(c):
+        def lane_block(j, carry):
+            at = c * CHUNK_PX + j * LANES
+            lanes = pl.ds(pl.multiple_of(at, LANES), LANES)
+            late = pl.ds(pl.multiple_of(pixel_count + at, LANES), LANES)
+            near = pl.ds(pl.multiple_of(j * LANES, LANES), LANES)
+            far = pl.ds(pl.multiple_of(CHUNK_PX + j * LANES, LANES), LANES)
+            hx, hy = halves(lanes)
+            cx, sx = step_table(hx)
+            cy, sy = step_table(hy)
+            for a in range(SIDE):
+                tc, ts = times((cx[a : a + 1], sx[a : a + 1]), (cy, sy))
+                tab_c[a * SIDE : (a + 1) * SIDE] = tc
+                tab_s[a * SIDE : (a + 1) * SIDE] = ts
+            re = mref[:, lanes].astype(jnp.float32)
+            im = mref[:, late].astype(jnp.float32)
+            for s in range(NSHIFT):
+                p = tab_c[s : s + 1]
+                q = tab_s[s : s + 1]
+                kern[s * refs : (s + 1) * refs, near] = (p * re - q * im).astype(jnp.bfloat16)
+                kern[s * refs : (s + 1) * refs, far] = (q * re + p * im).astype(jnp.bfloat16)
+            return carry
+
+        lax.fori_loop(0, CHUNK_BLOCKS, lane_block, 0)
+
+    tile = 256
+
+    def add_scores(c):
+        def row_block(j, carry):
+            at = pl.ds(pl.multiple_of(j * tile, tile), tile)
+            scores[at, :] += lax.dot_general(
+                kern[at, :],
+                rows[c],
+                (((1,), (1,)), ((), ())),
+                preferred_element_type=jnp.float32,
+            )
+            return carry
+
+        lax.fori_loop(0, NSHIFT * refs // tile, row_block, 0)
+
+    def gather_step(t, carry):
+        @pl.when(t + 2 < N_CHUNK)
+        def _():
+            for kind in range(3):
+                row_copy(kind, t + 2).start()
+
+        @pl.when(t < N_CHUNK)
+        def _():
+            row_copy(0, t).wait_recv()
+            row_copy(3, t).start()
+            row_copy(5, t).start()
+            row_copy(1, t).wait_recv()
+            row_copy(4, t).start()
+            row_copy(6, t).start()
+
+        @pl.when((t >= 1) & (t < N_CHUNK + 1))
+        def _():
+            row_copy(3, t - 1).wait_recv()
+            row_copy(7, t - 1).start()
+            row_copy(4, t - 1).wait_recv()
+            row_copy(8, t - 1).start()
+
+        @pl.when(t >= 2)
+        def _():
+            c = t - 2
+            make_kernels(c)
+            for kind in (2, 5, 6, 7, 8):
+                row_copy(kind, c).wait_recv()
+            add_scores(c)
+
+        return carry
+
+    lax.fori_loop(0, N_CHUNK + 2, gather_step, 0)
+
+    scale = 2.0 / math.sqrt(pixel_count)
+    top = jnp.max(scores[...], axis=0, keepdims=True) * scale
+    total = jnp.sum(jnp.exp(scores[...] * scale - top), axis=0, keepdims=True)
+    lbuf[me] = top + jnp.log(total)
+    for k in range(1, n_ori):
+        lse_copy(k).start()
+
+    seen = facts[...]
+    for k in range(1, n_ori):
+        fact_copy(k).wait_recv()
+        seen = seen + fbuf[k]
+    first, second, row_class = seen[0:1], seen[1:2], seen[2:3]
+    mine = (first == me) | (second == me)
+
+    for k in range(1, n_ori):
+        lse_copy(k).wait_recv()
+    peak = jnp.full(first.shape, -jnp.inf, jnp.float32)
+    for o in range(n_ori):
+        peak = jnp.where((first == o) | (second == o), jnp.maximum(peak, lbuf[o]), peak)
+    mass = jnp.zeros(first.shape, jnp.float32)
+    for o in range(n_ori):
+        mass += jnp.where((first == o) | (second == o), jnp.exp(lbuf[o] - peak), 0.0)
+    evidence = peak + jnp.log(mass)
+    ev_out[...] = evidence
+
+    def weigh(s, per_ref):
+        near = pl.ds(pl.multiple_of(s * refs, refs), refs)
+        far = pl.ds(pl.multiple_of((NSHIFT - 1 - s) * refs, refs), refs)
+        ahead = jnp.where(mine, jnp.exp(scores[near, :] * scale - evidence), 0.0)
+        behind = jnp.where(mine, jnp.exp(scores[far, :] * scale - evidence), 0.0)
+        both = ahead + behind
+        wp[near, :] = both.astype(jnp.bfloat16)
+        wm[near, :] = (ahead - behind).astype(jnp.bfloat16)
+        return per_ref + both
+
+    per_ref = lax.fori_loop(
+        0, HALF, weigh, jnp.zeros((refs, scores.shape[1]), jnp.float32), unroll=4
+    )
+    class_rows = lax.broadcasted_iota(jnp.int32, (LANES, scores.shape[1]), 0)
+    picks = (class_rows == row_class).astype(jnp.float32)
+    cbuf[0] = lax.dot_general(
+        per_ref,
+        picks,
+        (((1,), (1,)), ((), ())),
+        precision=lax.Precision.HIGHEST,
+        preferred_element_type=jnp.float32,
+    )
+
+    def back_block(i, b, h):
+        j = h * (n_grp * 8) + i * PIECE_BLOCKS + b
+        c = j // CHUNK_BLOCKS
+        off = lax.rem(j, CHUNK_BLOCKS) * LANES
+        lanes = pl.ds(pl.multiple_of(j * LANES, LANES), LANES)
+        hx, hy = halves(lanes)
+        cx, sx = times(step_table(hx), hx)
+        cy, sy = times(step_table(hy), hy)
+        for a in range(SIDE // 2):
+            tc, ts = times((cx[a : a + 1], sx[a : a + 1]), (cy, sy))
+            tab_c[a * SIDE : (a + 1) * SIDE] = tc
+            tab_s[a * SIDE : (a + 1) * SIDE] = ts
+        panel = jnp.concatenate(
+            [
+                rows[c, :, pl.ds(pl.multiple_of(off, LANES), LANES)],
+                rows[c, :, pl.ds(pl.multiple_of(CHUNK_PX + off, LANES), LANES)],
+            ],
+            axis=1,
+        )
+        even = jnp.dot(wp[...], panel, preferred_element_type=jnp.float32)
+        odd = jnp.dot(wm[...], panel, preferred_element_type=jnp.float32)
+        re = jnp.zeros((refs, LANES), jnp.float32)
+        im = jnp.zeros((refs, LANES), jnp.float32)
+        for s in range(HALF):
+            p = tab_c[s : s + 1]
+            q = tab_s[s : s + 1]
+            e = even[s * refs : (s + 1) * refs]
+            o = odd[s * refs : (s + 1) * refs]
+            re += p * e[:, :LANES] + q * o[:, LANES:]
+            im += p * e[:, LANES:] - q * o[:, :LANES]
+        hc, hs = times(hx, hy)
+        at = pl.ds(pl.multiple_of(b * LANES, LANES), LANES)
+        part[i, h, :, at] = hc * re - hs * im
+        part[i, 2 + h, :, at] = hc * im + hs * re
+
+    def back_piece(i, carry):
+        def one(n, inner):
+            back_block(i, n // 2, lax.rem(n, 2))
+            return inner
+
+        lax.fori_loop(0, 2 * PIECE_BLOCKS, one, 0)
+
+        @pl.when(i == 0)
+        def _():
+            for k in range(1, n_grp):
+                class_copy(k).start()
+
+        @pl.when(i > 0)
+        def _():
+            for k in range(1, n_grp):
+                back_copy(k, i - 1).start()
+
+        return carry
+
+    lax.fori_loop(0, PIECES, back_piece, 0)
+    for k in range(1, n_grp):
+        back_copy(k, PIECES - 1).start()
+
+    for k in range(1, n_grp):
+        class_copy(k).wait_recv()
+    class_out[...] = (cbuf[0] + cbuf[1]) + (cbuf[2] + cbuf[3])
+
+    wide = PIECE_BLOCKS * LANES
+
+    def finish(i, carry):
+        for k in range(1, n_grp):
+            back_copy(k, i).wait_recv()
+        at = pl.ds(pl.multiple_of(i * wide, LANES), wide)
+        back_out[:, at] = (part[i, g] + rbuf[1, i]) + (rbuf[2, i] + rbuf[3, i])
+        for k in range(1, n_grp):
+            back_copy(k, i).wait_send()
+        return carry
+
+    lax.fori_loop(0, PIECES, finish, 0)
+
+    def drain(c, carry):
+        for kind in range(9):
+            row_copy(kind, c).wait_send()
+        return carry
+
+    lax.fori_loop(0, N_CHUNK, drain, 0)
+    for k in range(1, n_ori):
+        fact_copy(k).wait_send()
+        lse_copy(k).wait_send()
+    for k in range(1, n_grp):
+        class_copy(k).wait_send()
+
+
+def per_device_fused(particles, priors, offsets, classes, ctf_table, references):
+    n_ori = lax.axis_size("ori")
+    n_grp = lax.axis_size("grp")
+    me = lax.axis_index("ori")
+    g = lax.axis_index("grp")
+    per = priors.shape[0]
+    refs = references.shape[0]
+    n_rows = n_ori * per
+    hyps = NSHIFT * refs
+    freq_x, freq_y = frequencies()
+    ax, ay = freq_x * (0.5 * two_pi / BOX), freq_y * (0.5 * two_pi / BOX)
+    base = jnp.stack([jnp.cos(ax), jnp.sin(ax), jnp.cos(ay), jnp.sin(ay)])
+    info = jnp.stack([classes, offsets[0], offsets[1]], axis=1)
+    listed = jnp.stack([priors[:, 0], priors[:, 1], classes])
+    listed = jnp.pad(listed, ((0, 5), (0, 0)))
+    placed = jnp.tile(listed, (1, n_ori))
+    facts = jnp.where(jnp.arange(n_rows)[None, :] // per == me, placed, 0)
+    wide = PIECES * PIECE_BLOCKS * LANES
+    vmem = pl.BlockSpec(memory_space=pltpu.VMEM)
+    sems = pltpu.SemaphoreType.DMA
+    back, by_class, evidence = pl.pallas_call(
+        functools.partial(fused_kernel, n_ori, n_grp),
+        out_shape=[
+            jax.ShapeDtypeStruct((refs, wide), jnp.float32),
+            jax.ShapeDtypeStruct((refs, LANES), jnp.float32),
+            jax.ShapeDtypeStruct((1, n_rows), jnp.float32),
+        ],
+        in_specs=[vmem] * 6,
+        out_specs=[vmem] * 3,
+        scratch_shapes=[
+            pltpu.VMEM((N_CHUNK, n_rows, 2 * CHUNK_PX), jnp.bfloat16),
+            pltpu.VMEM((hyps, 2 * CHUNK_PX), jnp.bfloat16),
+            pltpu.VMEM((hyps, n_rows), jnp.float32),
+            pltpu.VMEM((hyps // 2, n_rows), jnp.bfloat16),
+            pltpu.VMEM((hyps // 2, n_rows), jnp.bfloat16),
+            pltpu.VMEM((NSHIFT, LANES), jnp.float32),
+            pltpu.VMEM((NSHIFT, LANES), jnp.float32),
+            pltpu.VMEM((n_ori, 8, n_rows), jnp.int32),
+            pltpu.VMEM((n_ori, 1, n_rows), jnp.float32),
+            pltpu.VMEM((n_grp, refs, LANES), jnp.float32),
+            pltpu.VMEM((PIECES, n_grp, refs, PIECE_BLOCKS * LANES), jnp.float32),
+            pltpu.VMEM((n_grp, PIECES, refs, PIECE_BLOCKS * LANES), jnp.float32),
+            sems((9, N_CHUNK)),
+            sems((9, N_CHUNK)),
+            sems((n_ori,)),
+            sems((n_ori,)),
+            sems((n_ori,)),
+            sems((n_ori,)),
+            sems((n_grp,)),
+            sems((n_grp,)),
+            sems((n_grp, PIECES)),
+            sems((n_grp, PIECES)),
+        ],
+        compiler_params=pltpu.CompilerParams(
+            collective_id=0, has_side_effects=True, vmem_limit_bytes=56 * 2**20
+        ),
+    )(particles, info, facts, base, ctf_table, references)
+
+    n_classes = ctf_table.shape[0]
+    width = pixel_count // n_grp
+    table_part = lax.dynamic_slice_in_dim(ctf_table, g * width, width, 1)
+    weight_part = jnp.dot(
+        by_class[:, :n_classes], table_part * table_part, precision=lax.Precision.HIGHEST
+    )
+    cols = 2 * width
+    back_part = jnp.where(g % 2 == 0, back[:, :cols], back[:, wide - cols :])
+    own = lax.dynamic_slice_in_dim(evidence[0], me * per, per, 0)
+    return (back_part, weight_part, own)
+
+
 def solution(mesh):
+    small = mesh.shape["ori"] == 8 and mesh.shape["grp"] == 4
+    per_device = per_device_fused if small else per_device_plain
     placed = (
         P(("grp", "ori"), None),
         P(("grp", "ori"), None),

time: 174 us -> 121 us (0.70)
  Pallas kernels: 48.8 us -> 107 us
  waiting for transfers between devices: 50.8 us -> 0 us
  blocking collectives: 31.7 us -> 0 us
  between operations: 14.2 us -> 0.67 us
  other arithmetic: 19 us -> 6.64 us
  matrix products: 3.65 us -> 1.91 us
    pallas_call x2 -> x1, Pallas kernels: 48.8 us -> 107 us  [per_device_fused(): pl.pallas_call(functools.partial(fused_kernel, n_ori, n_grp), out_shape=[...]
    all_gather x1 -> x0, waiting for transfers between devices: 36.8 us -> none  [per_device(): rows = lax.all_gather(shifted, 'ori', axis=0, tiled=True)]
    all_gather x2 -> x0, blocking collectives: 19.4 us -> none  [the longest x1 10.6 us: per_device(): lax.all_gather(jnp.concatenate([priors, classes[:, None]], axis=1).T, 'or...]
    reduce_scatter x1 -> x0, waiting for transfers between devices: 14 us -> none  [per_device(): lax.psum_scatter(jnp.concatenate(pieces, axis=0), 'grp', scatter_dimensio...]
    psum x1 -> x0, blocking collectives: 12.3 us -> none  [per_device(): by_class = lax.psum(by_class, 'grp')]
    cos x3 -> x0, other arithmetic: 5.8 us -> none  [axis_table(): return (jnp.cos(angle), jnp.sin(angle))]
    add x4 -> x0, other arithmetic: 4.02 us -> none  [the longest x2 4.01 us: outer_table(): sine = sx[:, None] * cy[None] + cx[:, None] * sy[None]]
    another operation x0 -> x5, local copies, waits for them, and re-layouts: none -> 2.29 us  [the longest x2 1.45 us: per_device_fused(): info = jnp.stack([classes, offsets[0], offsets[1]], axis=1)]
  transfers between devices with their start and end apart: 2 -> 0, of which waited for: 2 -> 0; matrix products, arithmetic and copies ran while one was open for 7% -> 0% of each run, Pallas kernels for 0% -> 0%
where the time goes in v2:
time: 121 us; the launch traced here: 120 us
  Pallas kernels  107 us (88%)
  other arithmetic  6.64 us (5%)
  local copies, waits for them, and re-layouts  3.55 us (3%)
  matrix products  1.91 us (2%)
    pallas_call x1, Pallas kernels, per_device_fused(): pl.pallas_call(functools.partial(fused_kernel, n_ori, n_grp), out_shape=[...  107 us

profile of v2, /device:TPU:0, one launch (start us, length us, event | category | flops | bytes accessed | tf_op | source)
XLA Modules:
  0.0 120.3 jit_solution(7703034942980726627)
XLA Ops:
  0.7 0.8 slice_bitcast_fusion.1
  1.4 0.7 pad_add_fusion.1
  2.1 0.8 slice_bitcast_fusion.3
  2.8 0.7 pad_add_fusion
  3.5 0.7 copy.12.info
  4.2 0.1 tile.10
  4.3 0.6 broadcast_select_fusion.facts
  4.9 1.0 fusion.9
  5.9 1.0 fusion.7
  6.9 0.8 pad_maximum_fusion.base
  7.7 107.5 %shard_map.85 = (f32[16,4224]{1,0:T(8,128)}, f32[16,128]{1,0:T(8,128)}, f32[1,256]{1,0:T(1,128)}) custom-call(bf16[32,16640]{1,0:T(8,128)(2,1)} %prt.1, s32[32,3]{1,0:T(8,128)} %copy.12.info, s32[8,256]{1,0:T(8,128)} %broadcast_select_fusion.facts, f32[4,8320]{1,0:T(4,128)} %pad_maximum_fusion.base, f32[16,8320]{1,0:T(8,128)} %ctf.1, bf16[16,16640]{1,0:T(8,128)(2,1)} %mref.1), custom_call_target="tpu_custom_call" | custom-call | tf_op jit(solution)/shard_map/pallas_call | solution.py:698
  115.2 1.3 %dynamic-slice_bitcast_fusion = f32[32]{0:T(128)} fusion(f32[1,256]{1,0:T(1,128)} %get-tuple-element.8, s32[]{:T(128)S(6)} %select_n.97), kind=kLoop, calls=%fused_computation.28 | loop fusion | bytes 260 | tf_op jit(solution)/shard_map/dynamic_slice | solution.py:744
  116.5 1.9 %slice_select_fusion = f32[16,4160]{1,0:T(8,128)} fusion(f32[16,4224]{1,0:T(8,128)} %get-tuple-element.6, pred[]{:T(512)S(6)} %eq.18), kind=kLoop, calls=%fused_computation | loop fusion | flops 66560 | bytes 798721 | tf_op jit(solution)/shard_map/jit(_where)/select_n | solution.py:743
  118.4 1.9 %fusion = f32[16,2080]{1,0:T(8,128)} fusion(f32[16,8320]{1,0:T(8,128)} %ctf.1, s32[]{:T(128)S(6)} %select_n.96, f32[16,128]{1,0:T(8,128)} %get-tuple-element.7), kind=kOutput, calls=%fused_computation.2 | convolution fusion | flops 6423040 | bytes 280580 | tf_op jit(solution)/shard_map/dot_general | solution.py:739
  (3 shorter events, 0.0 us)

commit v3 on v2

--- a/solution.py
+++ b/solution.py
@@ -266,7 +266,18 @@
 CHUNK_BLOCKS = CHUNK_PX // LANES
 PIECES = 11
 PIECE_BLOCKS = 3
+AHEAD = 4
 MESH = pl.DeviceIdType.MESH
+
+
+def small_phase(x):
+    y = x * x
+    c = jnp.ones_like(y)
+    s = jnp.ones_like(y)
+    for n in (5, 4, 3, 2, 1):
+        c = 1.0 - y * c * (1.0 / ((2 * n - 1) * (2 * n)))
+        s = 1.0 - y * s * (1.0 / ((2 * n) * (2 * n + 1)))
+    return c, x * s
 
 
 def square(z):
@@ -305,7 +316,6 @@
     prt,
     info,
     facts,
-    base,
     ctf,
     mref,
     back_out,
@@ -322,7 +332,9 @@
     lbuf,
     cbuf,
     part,
+    sent,
     rbuf,
+    base,
     row_send,
     row_recv,
     f_send,
@@ -356,6 +368,15 @@
             barrier, inc=1, device_id=(lax.rem(g + k, n_grp), me), device_id_type=MESH
         )
 
+    pixel = lax.broadcasted_iota(jnp.int32, (1, pixel_count), 1).astype(jnp.float32)
+    row = jnp.floor((pixel + 0.5) * (1.0 / PY))
+    freq_y = pixel - row * PY
+    freq_x = jnp.where(row < PX // 2, row, row - PX)
+    for n, freq in enumerate((freq_x, freq_y)):
+        cosine, sine = small_phase(freq * (0.5 * two_pi / BOX))
+        base[2 * n : 2 * n + 1, :] = cosine
+        base[2 * n + 1 : 2 * n + 2, :] = sine
+
     def halves(lanes):
         return (
             (base[0:1, lanes], base[1:2, lanes]),
@@ -387,7 +408,11 @@
         ).astype(jnp.bfloat16)
         return carry
 
-    lax.fori_loop(0, N_CHUNK * CHUNK_BLOCKS, center_block, 0)
+    def center_chunk(c):
+        lax.fori_loop(c * CHUNK_BLOCKS, (c + 1) * CHUNK_BLOCKS, center_block, 0)
+
+    for c in range(2):
+        center_chunk(c)
 
     pl.semaphore_wait(barrier, n_ori - 1 + n_grp - 1)
 
@@ -449,7 +474,7 @@
     def back_copy(k, i):
         to = lax.rem(g + k, n_grp)
         return pltpu.make_async_remote_copy(
-            src_ref=part.at[i, to],
+            src_ref=sent.at[i, to],
             dst_ref=rbuf.at[k, i],
             send_sem=b_send.at[k, i],
             recv_sem=b_recv.at[k, i],
@@ -457,11 +482,18 @@
             device_id_type=MESH,
         )
 
-    for c in range(2):
-        for kind in range(3):
-            row_copy(kind, c).start()
+    for kind in range(3):
+        row_copy(kind, 0).start()
     for k in range(1, n_ori):
         fact_copy(k).start()
+
+    def early(c, carry):
+        center_chunk(c)
+        for kind in range(3):
+            row_copy(kind, c - 1).start()
+        return carry
+
+    lax.fori_loop(2, AHEAD + 1, early, 0)
 
     scores[...] = jnp.zeros_like(scores)
 
@@ -477,13 +509,13 @@
             cy, sy = step_table(hy)
             for a in range(SIDE):
                 tc, ts = times((cx[a : a + 1], sx[a : a + 1]), (cy, sy))
-                tab_c[a * SIDE : (a + 1) * SIDE] = tc
-                tab_s[a * SIDE : (a + 1) * SIDE] = ts
+                tab_c[0, a * SIDE : (a + 1) * SIDE] = tc
+                tab_s[0, a * SIDE : (a + 1) * SIDE] = ts
             re = mref[:, lanes].astype(jnp.float32)
             im = mref[:, late].astype(jnp.float32)
             for s in range(NSHIFT):
-                p = tab_c[s : s + 1]
-                q = tab_s[s : s + 1]
+                p = tab_c[0, s : s + 1]
+                q = tab_s[0, s : s + 1]
                 kern[s * refs : (s + 1) * refs, near] = (p * re - q * im).astype(jnp.bfloat16)
                 kern[s * refs : (s + 1) * refs, far] = (q * re + p * im).astype(jnp.bfloat16)
             return carry
@@ -503,13 +535,13 @@
             )
             return carry
 
-        lax.fori_loop(0, NSHIFT * refs // tile, row_block, 0)
+        lax.fori_loop(0, NSHIFT * refs // tile, row_block, 0, unroll=2)
 
     def gather_step(t, carry):
-        @pl.when(t + 2 < N_CHUNK)
+        @pl.when(t + AHEAD < N_CHUNK)
         def _():
             for kind in range(3):
-                row_copy(kind, t + 2).start()
+                row_copy(kind, t + AHEAD).start()
 
         @pl.when(t < N_CHUNK)
         def _():
@@ -526,6 +558,10 @@
             row_copy(7, t - 1).start()
             row_copy(4, t - 1).wait_recv()
             row_copy(8, t - 1).start()
+
+        @pl.when(t + AHEAD + 1 < N_CHUNK)
+        def _():
+            center_chunk(t + AHEAD + 1)
 
         @pl.when(t >= 2)
         def _():
@@ -597,8 +633,8 @@
         cy, sy = times(step_table(hy), hy)
         for a in range(SIDE // 2):
             tc, ts = times((cx[a : a + 1], sx[a : a + 1]), (cy, sy))
-            tab_c[a * SIDE : (a + 1) * SIDE] = tc
-            tab_s[a * SIDE : (a + 1) * SIDE] = ts
+            tab_c[h, a * SIDE : (a + 1) * SIDE] = tc
+            tab_s[h, a * SIDE : (a + 1) * SIDE] = ts
         panel = jnp.concatenate(
             [
                 rows[c, :, pl.ds(pl.multiple_of(off, LANES), LANES)],
@@ -611,23 +647,25 @@
         re = jnp.zeros((refs, LANES), jnp.float32)
         im = jnp.zeros((refs, LANES), jnp.float32)
         for s in range(HALF):
-            p = tab_c[s : s + 1]
-            q = tab_s[s : s + 1]
+            p = tab_c[h, s : s + 1]
+            q = tab_s[h, s : s + 1]
             e = even[s * refs : (s + 1) * refs]
             o = odd[s * refs : (s + 1) * refs]
             re += p * e[:, :LANES] + q * o[:, LANES:]
             im += p * e[:, LANES:] - q * o[:, :LANES]
         hc, hs = times(hx, hy)
         at = pl.ds(pl.multiple_of(b * LANES, LANES), LANES)
-        part[i, h, :, at] = hc * re - hs * im
-        part[i, 2 + h, :, at] = hc * im + hs * re
+        for d, sums in ((h, hc * re - hs * im), (2 + h, hc * im + hs * re)):
+            part[i, d, :, at] = sums
+            sent[i, d, :, at] = sums.astype(jnp.bfloat16)
 
     def back_piece(i, carry):
         def one(n, inner):
-            back_block(i, n // 2, lax.rem(n, 2))
+            back_block(i, n, 0)
+            back_block(i, n, 1)
             return inner
 
-        lax.fori_loop(0, 2 * PIECE_BLOCKS, one, 0)
+        lax.fori_loop(0, PIECE_BLOCKS, one, 0)
 
         @pl.when(i == 0)
         def _():
@@ -655,7 +693,8 @@
         for k in range(1, n_grp):
             back_copy(k, i).wait_recv()
         at = pl.ds(pl.multiple_of(i * wide, LANES), wide)
-        back_out[:, at] = (part[i, g] + rbuf[1, i]) + (rbuf[2, i] + rbuf[3, i])
+        got = [rbuf[k, i].astype(jnp.float32) for k in range(1, n_grp)]
+        back_out[:, at] = (part[i, g] + got[0]) + (got[1] + got[2])
         for k in range(1, n_grp):
             back_copy(k, i).wait_send()
         return carry
@@ -684,9 +723,6 @@
     refs = references.shape[0]
     n_rows = n_ori * per
     hyps = NSHIFT * refs
-    freq_x, freq_y = frequencies()
-    ax, ay = freq_x * (0.5 * two_pi / BOX), freq_y * (0.5 * two_pi / BOX)
-    base = jnp.stack([jnp.cos(ax), jnp.sin(ax), jnp.cos(ay), jnp.sin(ay)])
     info = jnp.stack([classes, offsets[0], offsets[1]], axis=1)
     listed = jnp.stack([priors[:, 0], priors[:, 1], classes])
     listed = jnp.pad(listed, ((0, 5), (0, 0)))
@@ -702,7 +738,7 @@
             jax.ShapeDtypeStruct((refs, LANES), jnp.float32),
             jax.ShapeDtypeStruct((1, n_rows), jnp.float32),
         ],
-        in_specs=[vmem] * 6,
+        in_specs=[vmem] * 5,
         out_specs=[vmem] * 3,
         scratch_shapes=[
             pltpu.VMEM((N_CHUNK, n_rows, 2 * CHUNK_PX), jnp.bfloat16),
@@ -710,13 +746,15 @@
             pltpu.VMEM((hyps, n_rows), jnp.float32),
             pltpu.VMEM((hyps // 2, n_rows), jnp.bfloat16),
             pltpu.VMEM((hyps // 2, n_rows), jnp.bfloat16),
-            pltpu.VMEM((NSHIFT, LANES), jnp.float32),
-            pltpu.VMEM((NSHIFT, LANES), jnp.float32),
+            pltpu.VMEM((2, NSHIFT, LANES), jnp.float32),
+            pltpu.VMEM((2, NSHIFT, LANES), jnp.float32),
             pltpu.VMEM((n_ori, 8, n_rows), jnp.int32),
             pltpu.VMEM((n_ori, 1, n_rows), jnp.float32),
             pltpu.VMEM((n_grp, refs, LANES), jnp.float32),
             pltpu.VMEM((PIECES, n_grp, refs, PIECE_BLOCKS * LANES), jnp.float32),
-            pltpu.VMEM((n_grp, PIECES, refs, PIECE_BLOCKS * LANES), jnp.float32),
+            pltpu.VMEM((PIECES, n_grp, refs, PIECE_BLOCKS * LANES), jnp.bfloat16),
+            pltpu.VMEM((n_grp, PIECES, refs, PIECE_BLOCKS * LANES), jnp.bfloat16),
+            pltpu.VMEM((4, pixel_count), jnp.float32),
             sems((9, N_CHUNK)),
             sems((9, N_CHUNK)),
             sems((n_ori,)),
@@ -731,7 +769,7 @@
         compiler_params=pltpu.CompilerParams(
             collective_id=0, has_side_effects=True, vmem_limit_bytes=56 * 2**20
         ),
-    )(particles, info, facts, base, ctf_table, references)
+    )(particles, info, facts, ctf_table, references)
 
     n_classes = ctf_table.shape[0]
     width = pixel_count // n_grp

time: 121 us -> 100 us (0.83)
  Pallas kernels: 107 us -> 90.1 us
  other arithmetic: 6.64 us -> 3.82 us
    pallas_call x1, Pallas kernels: 107 us -> 90.1 us  [per_device_fused(): pl.pallas_call(functools.partial(fused_kernel, n_ori, n_grp), out_shape=[...]
    sin x2 -> x0, other arithmetic: 2.04 us -> none  [per_device_fused(): base = jnp.stack([jnp.cos(ax), jnp.sin(ax), jnp.cos(ay), jnp.sin(ay)])]
where the time goes in v3:
time: 100 us
  Pallas kernels  90.1 us (90%)
  other arithmetic  3.82 us (4%)
  local copies, waits for them, and re-layouts  3.49 us (3%)
  matrix products  1.91 us (2%)
    pallas_call x1, Pallas kernels, per_device_fused(): pl.pallas_call(functools.partial(fused_kernel, n_ori, n_grp), out_shape=[...  90.1 us

profile of v3, /device:TPU:0, one launch (start us, length us, event | category | flops | bytes accessed | tf_op | source)
XLA Modules:
  0.0 100.0 jit_solution(9546721970779453262)
XLA Ops:
  0.7 0.8 slice_bitcast_fusion.1
  1.4 0.7 pad_add_fusion.1
  2.1 0.8 slice_bitcast_fusion.3
  2.8 0.7 pad_add_fusion
  3.5 0.7 copy.12.info
  4.2 0.1 tile.10
  4.3 0.6 broadcast_select_fusion.facts
  4.9 90.1 %shard_map.85 = (f32[16,4224]{1,0:T(8,128)}, f32[16,128]{1,0:T(8,128)}, f32[1,256]{1,0:T(1,128)}) custom-call(bf16[32,16640]{1,0:T(8,128)(2,1)} %prt.1, s32[32,3]{1,0:T(8,128)} %copy.12.info, s32[8,256]{1,0:T(8,128)} %broadcast_select_fusion.facts, f32[16,8320]{1,0:T(8,128)} %ctf.1, bf16[16,16640]{1,0:T(8,128)(2,1)} %mref.1), custom_call_target="tpu_custom_call" | custom-call | tf_op jit(solution)/shard_map/pallas_call | solution.py:734
  95.0 1.2 %dynamic-slice_bitcast_fusion = f32[32]{0:T(128)} fusion(f32[1,256]{1,0:T(1,128)} %get-tuple-element.8, s32[]{:T(128)S(6)} %select_n.41), kind=kLoop, calls=%fused_computation.13 | loop fusion | bytes 260 | tf_op jit(solution)/shard_map/dynamic_slice | solution.py:782
  96.2 1.9 %slice_select_fusion = f32[16,4160]{1,0:T(8,128)} fusion(f32[16,4224]{1,0:T(8,128)} %get-tuple-element.6, pred[]{:T(512)S(6)} %eq.16), kind=kLoop, calls=%fused_computation | loop fusion | flops 66560 | bytes 798721 | tf_op jit(solution)/shard_map/jit(_where)/select_n | solution.py:781
  98.1 1.9 %fusion = f32[16,2080]{1,0:T(8,128)} fusion(f32[16,8320]{1,0:T(8,128)} %ctf.1, s32[]{:T(128)S(6)} %select_n.40, f32[16,128]{1,0:T(8,128)} %get-tuple-element.7), kind=kOutput, calls=%fused_computation.1 | convolution fusion | flops 6423040 | bytes 280580 | tf_op jit(solution)/shard_map/dot_general | solution.py:777
  (3 shorter events, 0.0 us)
